TPU v7x, 256 devices: a whole 4x4x8 slice. The times are simulated.
256 devices in a mesh: section: 16 (over x, y), col: 16 (over z, core).
Axes of the slice: x: 4, y: 4, z: 8, core: 2. Of those that a mesh axis runs over, the one named last changes fastest.
Arguments:
- features: bfloat16 [4, 32, 65536], P(None, 'section', 'col'), may hold values from -48 to 48
- weights: bfloat16 [16, 512, 4, 128, 128], P('section', 'col'), may hold values from -0.375 to 0.375
- sources: int32 [16, 512, 4], P('section', 'col'), may hold values from 0 to 511, as said below
- bias: float32 [16, 65536], P('section', 'col'), may hold values from -0.3 to 0.3
- batch_rows: int32 [4], replicated, may hold values from 1 to 32, as said below
Outputs:
- final_act: bfloat16 [4, 32, 65536], P(None, 'section', 'col')
Inputs may be any that keep to these rules, and one draw needn't show every extreme that they name: In every layer, the sources of all block columns c with c // 32 = d name exactly 2 distinct blocks b with b // 32 = e, for every pair d, e. `batch_rows`: some micro-batch has exactly 32 live rows.
All inputs are finite; a program needn't handle non-finite values.
Results may differ from a plain program's by a relative error of at most 0.033.
Values may be sent and summed in bfloat16 or wider, within the bound.
A program may use at most 64 MiB of HBM per device.

v0:
```python
import jax
import jax.numpy as jnp
from jax import lax
from jax.sharding import PartitionSpec as P

CAP = 2


def from_behind(x, axis, by):
    size = lax.axis_size(axis)
    pairs = [(i, i + by) for i in range(size) if 0 <= i + by < size]
    return lax.ppermute(x, axis, pairs)


def request_lists(pattern_table, owners, blocks_own, slot_total):
    dest_entries = pattern_table.reshape(owners, -1)
    block_total = owners * blocks_own
    catalog = jnp.arange(block_total, dtype=jnp.int32)
    wanted = jnp.any(dest_entries[:, :, None] == catalog[None, None, :], axis=1)
    wanted = wanted.reshape(owners, owners, blocks_own)
    block_ranks = jnp.cumsum(wanted.astype(jnp.int32), axis=2) - 1
    slot_ids = jnp.arange(slot_total, dtype=jnp.int32)
    chosen = wanted[:, :, None, :] & (block_ranks[:, :, None, :] == slot_ids[None, None, :, None])
    local_ids = jnp.arange(blocks_own, dtype=jnp.int32)
    positions = jnp.sum(chosen.astype(jnp.int32) * local_ids[None, None, None, :], axis=3)
    present = jnp.any(chosen, axis=3)
    return (positions, present)


def body(features, weights, sources, bias, batch_rows):
    sections = lax.axis_size("section")
    owners = lax.axis_size("col")
    section_idx = lax.axis_index("section")
    col_idx = lax.axis_index("col")
    local_w = weights[0]
    blocks_own = local_w.shape[0]
    nonzero_count = local_w.shape[1]
    block_size = local_w.shape[2]
    local_src = sources[0].reshape(blocks_own * nonzero_count)
    local_bias = bias[0].reshape(blocks_own, 1, block_size)
    pattern_table = lax.all_gather(sources[0], "col", axis=0, tiled=True)
    positions, present = request_lists(pattern_table, owners, blocks_own, CAP)
    outgoing = lax.dynamic_index_in_dim(positions, col_idx, 1, keepdims=False).reshape(owners * CAP)
    incoming = lax.dynamic_index_in_dim(positions, col_idx, 0, keepdims=False)
    incoming_ok = lax.dynamic_index_in_dim(present, col_idx, 0, keepdims=False)
    global_ids = incoming + blocks_own * jnp.arange(owners, dtype=jnp.int32)[:, None]
    matches = (local_src[:, None] == global_ids.reshape(-1)[None, :]) & incoming_ok.reshape(-1)[
        None, :
    ]
    slot_of = jnp.sum(
        matches.astype(jnp.int32) * jnp.arange(owners * CAP, dtype=jnp.int32)[None, :], axis=1
    )
    all_inputs = lax.all_gather(features, "section", axis=1, tiled=True)
    batches = all_inputs.shape[0]
    row_total = all_inputs.shape[1]
    pieces = 1
    part_rows = row_total // pieces
    piece_total = batches * pieces
    tick_total = piece_total + sections - 1
    blocks_in = all_inputs.reshape(batches, pieces, part_rows, blocks_own, block_size)
    blocks_in = blocks_in.transpose(0, 1, 3, 2, 4).reshape(
        piece_total, blocks_own, part_rows, block_size
    )

    def combine(received):
        rows_here = received.shape[2]
        flat_recv = received.reshape(owners * CAP, rows_here, block_size)
        picked = jnp.take(flat_recv, slot_of, axis=0).reshape(
            blocks_own, nonzero_count, rows_here, block_size
        )
        preact = jnp.einsum("ckrb,ckbo->cro", picked, local_w, preferred_element_type=jnp.float32)
        return jnp.clip(preact + local_bias, 0.0, 32.0).astype(jnp.bfloat16)

    def apply_layer(carried):
        payload = jnp.take(carried, outgoing, axis=0).reshape(
            owners, CAP, carried.shape[1], block_size
        )
        return combine(lax.all_to_all(payload, "col", split_axis=0, concat_axis=0, tiled=True))

    def tick(tick_idx, carry):
        carried, finished = carry
        entering = lax.dynamic_index_in_dim(
            blocks_in, jnp.minimum(tick_idx, piece_total - 1), 0, keepdims=False
        )
        current = jnp.where(section_idx == 0, entering, carried)
        layer_out = apply_layer(current)
        slot_idx = jnp.clip(tick_idx - sections + 1, 0, piece_total - 1)
        storing = (section_idx == sections - 1) & (tick_idx >= sections - 1)
        existing = lax.dynamic_index_in_dim(finished, slot_idx, 0, keepdims=False)
        finished = lax.dynamic_update_index_in_dim(
            finished, jnp.where(storing, layer_out, existing), slot_idx, 0
        )
        passed = from_behind(layer_out, "section", 1)
        return (passed, finished)

    initial = (
        jnp.zeros((blocks_own, part_rows, block_size), jnp.bfloat16),
        jnp.zeros((piece_total, blocks_own, part_rows, block_size), jnp.bfloat16),
    )
    carried, finished = lax.fori_loop(0, tick_total, tick, initial)
    completed = finished.reshape(batches, pieces, blocks_own, part_rows, block_size)
    completed = completed.transpose(0, 1, 3, 2, 4).reshape(
        batches, row_total, blocks_own * block_size
    )
    own_rows = row_total // sections
    outgoing_rows = completed.reshape(batches, sections, own_rows, blocks_own * block_size)
    gathered = lax.all_to_all(outgoing_rows, "section", split_axis=1, concat_axis=1, tiled=True)
    own_result = gathered[:, sections - 1]
    row_ids = section_idx * own_rows + jnp.arange(own_rows, dtype=jnp.int32)
    row_mask = row_ids[None, :] < batch_rows[:, None]
    return jnp.where(row_mask[:, :, None], own_result, jnp.zeros_like(own_result))


def solution(mesh):
    in_specs = (
        P(None, "section", "col"),
        P("section", "col", None, None, None),
        P("section", "col", None),
        P("section", "col"),
        P(),
    )
    out_specs = P(None, "section", "col")
    return jax.shard_map(body, mesh=mesh, in_specs=in_specs, out_specs=out_specs, check_vma=False)
```

profile of v0, /device:TPU:8, one launch (start us, length us, event | category | flops | bytes accessed | tf_op | source)
XLA Modules:
  0.0 745.7 jit_solution(5742801372019623297)
XLA Ops:
  9.9 20.7 %all-gather = s32[1,512,4]{2,0,1:T(1,128)S(1)} all-gather(s32[1,32,4]{2,0,1:T(1,128)S(1)} %copy.19), channel_id=2, replica_groups=mesh['section'=16,'col'=16] {'col'}, dimensions={1}, use_global_device_ids=true | all-gather | bytes 8704 | tf_op jit(solution)/shard_map/all_gather | solution.py:41
  38.9 21.1 %all-gather.3.cloned.1.call-done = bf16[4,32,4096]{2,0,1:T(4,128)(2,1)} async-done(((bf16[4,2,4096]{2,0,1:T(4,128)(2,1)}), bf16[4,32,4096]{2,0,1:T(4,128)(2,1)}) %all-gather.3.cloned.1.call-update) | async-done | bytes 1048592 | tf_op jit(solution)/shard_map/all_gather | solution.py:53
  63.2 641.0 %while.19 = (s32[]{:T(128)}, bf16[32,32,128]{2,1,0:T(8,128)(2,1)S(1)}, bf16[4,32,32,128]{3,2,1,0:T(8,128)(2,1)S(1)}, s32[128]{0:T(128)S(1)}, s32[32]{0:T(128)S(1...) while((s32[]{:T(128)}, ...), condition=%wide.region_6.7_spmd, body=%wide.region_5.6_spmd.sunk | while | flops 135531952 | bytes 12878729 | solution.py:100
  65.9 7.1 all-to-all-start
  73.2 11.0 %all-to-all-done = bf16[16,2,32,128]{3,2,1,0:T(8,128)(2,1)S(1)} async-done(((bf16[16,2,32,128]{3,2,1,0:T(8,128)(2,1)}), bf16[16,2,32,128]{3,2,1,0:T(8,128)(2,1)S(1)}, u32[]{:S(2)}, u32[]{:S(2)}) %all-to-all-start) | async-done | bytes 262176 | tf_op jit(solution)/shard_map/while/body/eval_jaxpr/all_to_all | solution.py:78
  91.2 7.8 %collective-permute-done = bf16[32,32,128]{2,1,0:T(8,128)(2,1)S(1)} collective-permute-done((bf16[32,32,128]{2,1,0:T(8,128)(2,1)S(1)}, bf16[32,32,128]{2,1,0:T(8,128)(2,1)S(1)}, u32[]{:S(2)}, u32[]{:S(2)}) %collective-permute-start) | collective-permute-done | bytes 262176 | tf_op jit(solution)/shard_map/while/body/eval_jaxpr/ppermute | solution.py:12
  105.4 10.8 %all-to-all-done = bf16[16,2,32,128]{3,2,1,0:T(8,128)(2,1)S(1)} async-done(((bf16[16,2,32,128]{3,2,1,0:T(8,128)(2,1)}), bf16[16,2,32,128]{3,2,1,0:T(8,128)(2,1)S(1)}, u32[]{:S(2)}, u32[]{:S(2)}) %all-to-all-start) | async-done | bytes 262176 | tf_op jit(solution)/shard_map/while/body/eval_jaxpr/all_to_all | solution.py:78
  123.3 7.7 %collective-permute-done = bf16[32,32,128]{2,1,0:T(8,128)(2,1)S(1)} collective-permute-done((bf16[32,32,128]{2,1,0:T(8,128)(2,1)S(1)}, bf16[32,32,128]{2,1,0:T(8,128)(2,1)S(1)}, u32[]{:S(2)}, u32[]{:S(2)}) %collective-permute-start) | collective-permute-done | bytes 262176 | tf_op jit(solution)/shard_map/while/body/eval_jaxpr/ppermute | solution.py:12
  137.3 10.8 %all-to-all-done = bf16[16,2,32,128]{3,2,1,0:T(8,128)(2,1)S(1)} async-done(((bf16[16,2,32,128]{3,2,1,0:T(8,128)(2,1)}), bf16[16,2,32,128]{3,2,1,0:T(8,128)(2,1)S(1)}, u32[]{:S(2)}, u32[]{:S(2)}) %all-to-all-start) | async-done | bytes 262176 | tf_op jit(solution)/shard_map/while/body/eval_jaxpr/all_to_all | solution.py:78
  155.2 7.7 %collective-permute-done = bf16[32,32,128]{2,1,0:T(8,128)(2,1)S(1)} collective-permute-done((bf16[32,32,128]{2,1,0:T(8,128)(2,1)S(1)}, bf16[32,32,128]{2,1,0:T(8,128)(2,1)S(1)}, u32[]{:S(2)}, u32[]{:S(2)}) %collective-permute-start) | collective-permute-done | bytes 262176 | tf_op jit(solution)/shard_map/while/body/eval_jaxpr/ppermute | solution.py:12
  169.3 10.8 %all-to-all-done = bf16[16,2,32,128]{3,2,1,0:T(8,128)(2,1)S(1)} async-done(((bf16[16,2,32,128]{3,2,1,0:T(8,128)(2,1)}), bf16[16,2,32,128]{3,2,1,0:T(8,128)(2,1)S(1)}, u32[]{:S(2)}, u32[]{:S(2)}) %all-to-all-start) | async-done | bytes 262176 | tf_op jit(solution)/shard_map/while/body/eval_jaxpr/all_to_all | solution.py:78
  187.2 7.6 %collective-permute-done = bf16[32,32,128]{2,1,0:T(8,128)(2,1)S(1)} collective-permute-done((bf16[32,32,128]{2,1,0:T(8,128)(2,1)S(1)}, bf16[32,32,128]{2,1,0:T(8,128)(2,1)S(1)}, u32[]{:S(2)}, u32[]{:S(2)}) %collective-permute-start) | collective-permute-done | bytes 262176 | tf_op jit(solution)/shard_map/while/body/eval_jaxpr/ppermute | solution.py:12
  201.2 10.8 %all-to-all-done = bf16[16,2,32,128]{3,2,1,0:T(8,128)(2,1)S(1)} async-done(((bf16[16,2,32,128]{3,2,1,0:T(8,128)(2,1)}), bf16[16,2,32,128]{3,2,1,0:T(8,128)(2,1)S(1)}, u32[]{:S(2)}, u32[]{:S(2)}) %all-to-all-start) | async-done | bytes 262176 | tf_op jit(solution)/shard_map/while/body/eval_jaxpr/all_to_all | solution.py:78
  234.0 10.8 %all-to-all-done = bf16[16,2,32,128]{3,2,1,0:T(8,128)(2,1)S(1)} async-done(((bf16[16,2,32,128]{3,2,1,0:T(8,128)(2,1)}), bf16[16,2,32,128]{3,2,1,0:T(8,128)(2,1)S(1)}, u32[]{:S(2)}, u32[]{:S(2)}) %all-to-all-start) | async-done | bytes 262176 | tf_op jit(solution)/shard_map/while/body/eval_jaxpr/all_to_all | solution.py:78
  248.7 6.5 collective-permute-start
  268.0 10.8 %all-to-all-done = bf16[16,2,32,128]{3,2,1,0:T(8,128)(2,1)S(1)} async-done(((bf16[16,2,32,128]{3,2,1,0:T(8,128)(2,1)}), bf16[16,2,32,128]{3,2,1,0:T(8,128)(2,1)S(1)}, u32[]{:S(2)}, u32[]{:S(2)}) %all-to-all-start) | async-done | bytes 262176 | tf_op jit(solution)/shard_map/while/body/eval_jaxpr/all_to_all | solution.py:78
  282.7 6.5 collective-permute-start
  302.1 10.8 %all-to-all-done = bf16[16,2,32,128]{3,2,1,0:T(8,128)(2,1)S(1)} async-done(((bf16[16,2,32,128]{3,2,1,0:T(8,128)(2,1)}), bf16[16,2,32,128]{3,2,1,0:T(8,128)(2,1)S(1)}, u32[]{:S(2)}, u32[]{:S(2)}) %all-to-all-start) | async-done | bytes 262176 | tf_op jit(solution)/shard_map/while/body/eval_jaxpr/all_to_all | solution.py:78
  316.7 6.5 collective-permute-start
  336.1 10.8 %all-to-all-done = bf16[16,2,32,128]{3,2,1,0:T(8,128)(2,1)S(1)} async-done(((bf16[16,2,32,128]{3,2,1,0:T(8,128)(2,1)}), bf16[16,2,32,128]{3,2,1,0:T(8,128)(2,1)S(1)}, u32[]{:S(2)}, u32[]{:S(2)}) %all-to-all-start) | async-done | bytes 262176 | tf_op jit(solution)/shard_map/while/body/eval_jaxpr/all_to_all | solution.py:78
  370.2 10.8 %all-to-all-done = bf16[16,2,32,128]{3,2,1,0:T(8,128)(2,1)S(1)} async-done(((bf16[16,2,32,128]{3,2,1,0:T(8,128)(2,1)}), bf16[16,2,32,128]{3,2,1,0:T(8,128)(2,1)S(1)}, u32[]{:S(2)}, u32[]{:S(2)}) %all-to-all-start) | async-done | bytes 262176 | tf_op jit(solution)/shard_map/while/body/eval_jaxpr/all_to_all | solution.py:78
  404.2 10.8 %all-to-all-done = bf16[16,2,32,128]{3,2,1,0:T(8,128)(2,1)S(1)} async-done(((bf16[16,2,32,128]{3,2,1,0:T(8,128)(2,1)}), bf16[16,2,32,128]{3,2,1,0:T(8,128)(2,1)S(1)}, u32[]{:S(2)}, u32[]{:S(2)}) %all-to-all-start) | async-done | bytes 262176 | tf_op jit(solution)/shard_map/while/body/eval_jaxpr/all_to_all | solution.py:78
  438.2 10.8 %all-to-all-done = bf16[16,2,32,128]{3,2,1,0:T(8,128)(2,1)S(1)} async-done(((bf16[16,2,32,128]{3,2,1,0:T(8,128)(2,1)}), bf16[16,2,32,128]{3,2,1,0:T(8,128)(2,1)S(1)}, u32[]{:S(2)}, u32[]{:S(2)}) %all-to-all-start) | async-done | bytes 262176 | tf_op jit(solution)/shard_map/while/body/eval_jaxpr/all_to_all | solution.py:78
  472.3 10.8 %all-to-all-done = bf16[16,2,32,128]{3,2,1,0:T(8,128)(2,1)S(1)} async-done(((bf16[16,2,32,128]{3,2,1,0:T(8,128)(2,1)}), bf16[16,2,32,128]{3,2,1,0:T(8,128)(2,1)S(1)}, u32[]{:S(2)}, u32[]{:S(2)}) %all-to-all-start) | async-done | bytes 262176 | tf_op jit(solution)/shard_map/while/body/eval_jaxpr/all_to_all | solution.py:78
  506.3 10.8 %all-to-all-done = bf16[16,2,32,128]{3,2,1,0:T(8,128)(2,1)S(1)} async-done(((bf16[16,2,32,128]{3,2,1,0:T(8,128)(2,1)}), bf16[16,2,32,128]{3,2,1,0:T(8,128)(2,1)S(1)}, u32[]{:S(2)}, u32[]{:S(2)}) %all-to-all-start) | async-done | bytes 262176 | tf_op jit(solution)/shard_map/while/body/eval_jaxpr/all_to_all | solution.py:78
  540.4 10.8 %all-to-all-done = bf16[16,2,32,128]{3,2,1,0:T(8,128)(2,1)S(1)} async-done(((bf16[16,2,32,128]{3,2,1,0:T(8,128)(2,1)}), bf16[16,2,32,128]{3,2,1,0:T(8,128)(2,1)S(1)}, u32[]{:S(2)}, u32[]{:S(2)}) %all-to-all-start) | async-done | bytes 262176 | tf_op jit(solution)/shard_map/while/body/eval_jaxpr/all_to_all | solution.py:78
  574.4 10.8 %all-to-all-done = bf16[16,2,32,128]{3,2,1,0:T(8,128)(2,1)S(1)} async-done(((bf16[16,2,32,128]{3,2,1,0:T(8,128)(2,1)}), bf16[16,2,32,128]{3,2,1,0:T(8,128)(2,1)S(1)}, u32[]{:S(2)}, u32[]{:S(2)}) %all-to-all-start) | async-done | bytes 262176 | tf_op jit(solution)/shard_map/while/body/eval_jaxpr/all_to_all | solution.py:78
  608.4 10.8 %all-to-all-done = bf16[16,2,32,128]{3,2,1,0:T(8,128)(2,1)S(1)} async-done(((bf16[16,2,32,128]{3,2,1,0:T(8,128)(2,1)}), bf16[16,2,32,128]{3,2,1,0:T(8,128)(2,1)S(1)}, u32[]{:S(2)}, u32[]{:S(2)}) %all-to-all-start) | async-done | bytes 262176 | tf_op jit(solution)/shard_map/while/body/eval_jaxpr/all_to_all | solution.py:78
  642.5 10.8 %all-to-all-done = bf16[16,2,32,128]{3,2,1,0:T(8,128)(2,1)S(1)} async-done(((bf16[16,2,32,128]{3,2,1,0:T(8,128)(2,1)}), bf16[16,2,32,128]{3,2,1,0:T(8,128)(2,1)S(1)}, u32[]{:S(2)}, u32[]{:S(2)}) %all-to-all-start) | async-done | bytes 262176 | tf_op jit(solution)/shard_map/while/body/eval_jaxpr/all_to_all | solution.py:78
  676.5 10.8 %all-to-all-done = bf16[16,2,32,128]{3,2,1,0:T(8,128)(2,1)S(1)} async-done(((bf16[16,2,32,128]{3,2,1,0:T(8,128)(2,1)}), bf16[16,2,32,128]{3,2,1,0:T(8,128)(2,1)S(1)}, u32[]{:S(2)}, u32[]{:S(2)}) %all-to-all-start) | async-done | bytes 262176 | tf_op jit(solution)/shard_map/while/body/eval_jaxpr/all_to_all | solution.py:78
  707.0 14.3 %all-to-all-start.1 = ((bf16[4,16,2,4096]{3,2,0,1:T(2,128)(2,1)}), bf16[4,16,2,4096]{3,2,0,1:T(2,128)(2,1)S(1)}, u32[]{:S(2)}, u32[]{:S(2)}) async-start(bf16[4,16,2,4096]{3,2,0,1:T(2,128)(2,1)} %copy.26), calls=%async_computation.1 | async-start | bytes 2097152 | tf_op jit(solution)/shard_map/all_to_all | solution.py:107
  721.5 16.6 %all-to-all-done.1 = bf16[4,16,2,4096]{3,2,0,1:T(2,128)(2,1)S(1)} async-done(((bf16[4,16,2,4096]{3,2,0,1:T(2,128)(2,1)}), bf16[4,16,2,4096]{3,2,0,1:T(2,128)(2,1)S(1)}, u32[]{:S(2)}, u32[]{:S(2)}) %all-to-all-start.1) | async-done | bytes 1048608 | tf_op jit(solution)/shard_map/all_to_all | solution.py:107
  (376 shorter events, 394.4 us)
Async XLA Ops:
  6.5 53.5 %all-gather.3.cloned.1.call-start = ((), (), s32[]{:S(2)}) async-start(), calls=%async_computation.2 | async-start | bytes 1114112 | tf_op jit(solution)/shard_map/all_gather | solution.py:53
  65.9 18.3 %all-to-all-start = ((bf16[16,2,32,128]{3,2,1,0:T(8,128)(2,1)}), bf16[16,2,32,128]{3,2,1,0:T(8,128)(2,1)S(1)}, u32[]{:S(2)}, u32[]{:S(2)}) async-start(bf16[16,2,32,128]{3,2,1,0:T(8,128)(2,1)} %broadcast_select_fusion.3), calls=%async_computation | async-start | bytes 524288 | tf_op jit(solution)/shard_map/while/body/eval_jaxpr/all_to_all | solution.py:78
  101.7 14.5 %all-to-all-start = ((bf16[16,2,32,128]{3,2,1,0:T(8,128)(2,1)}), bf16[16,2,32,128]{3,2,1,0:T(8,128)(2,1)S(1)}, u32[]{:S(2)}, u32[]{:S(2)}) async-start(bf16[16,2,32,128]{3,2,1,0:T(8,128)(2,1)} %broadcast_select_fusion.3), calls=%async_computation | async-start | bytes 524288 | tf_op jit(solution)/shard_map/while/body/eval_jaxpr/all_to_all | solution.py:78
  133.6 14.5 %all-to-all-start = ((bf16[16,2,32,128]{3,2,1,0:T(8,128)(2,1)}), bf16[16,2,32,128]{3,2,1,0:T(8,128)(2,1)S(1)}, u32[]{:S(2)}, u32[]{:S(2)}) async-start(bf16[16,2,32,128]{3,2,1,0:T(8,128)(2,1)} %broadcast_select_fusion.3), calls=%async_computation | async-start | bytes 524288 | tf_op jit(solution)/shard_map/while/body/eval_jaxpr/all_to_all | solution.py:78
  165.5 14.5 %all-to-all-start = ((bf16[16,2,32,128]{3,2,1,0:T(8,128)(2,1)}), bf16[16,2,32,128]{3,2,1,0:T(8,128)(2,1)S(1)}, u32[]{:S(2)}, u32[]{:S(2)}) async-start(bf16[16,2,32,128]{3,2,1,0:T(8,128)(2,1)} %broadcast_select_fusion.3), calls=%async_computation | async-start | bytes 524288 | tf_op jit(solution)/shard_map/while/body/eval_jaxpr/all_to_all | solution.py:78
  197.5 14.5 %all-to-all-start = ((bf16[16,2,32,128]{3,2,1,0:T(8,128)(2,1)}), bf16[16,2,32,128]{3,2,1,0:T(8,128)(2,1)S(1)}, u32[]{:S(2)}, u32[]{:S(2)}) async-start(bf16[16,2,32,128]{3,2,1,0:T(8,128)(2,1)} %broadcast_select_fusion.3), calls=%async_computation | async-start | bytes 524288 | tf_op jit(solution)/shard_map/while/body/eval_jaxpr/all_to_all | solution.py:78
  230.3 14.5 %all-to-all-start = ((bf16[16,2,32,128]{3,2,1,0:T(8,128)(2,1)}), bf16[16,2,32,128]{3,2,1,0:T(8,128)(2,1)S(1)}, u32[]{:S(2)}, u32[]{:S(2)}) async-start(bf16[16,2,32,128]{3,2,1,0:T(8,128)(2,1)} %broadcast_select_fusion.3), calls=%async_computation | async-start | bytes 524288 | tf_op jit(solution)/shard_map/while/body/eval_jaxpr/all_to_all | solution.py:78
  248.7 13.0 %collective-permute-start = (bf16[32,32,128]{2,1,0:T(8,128)(2,1)S(1)}, bf16[32,32,128]{2,1,0:T(8,128)(2,1)S(1)}, u32[]{:S(2)}, u32[]{:S(2)}) collective-permute-start(bf16[32,32,128]{2,1,0:T(8,128)(2,1)S(1)} %get-tuple-element.421), channel_id=1, source_target_pairs={{0,16},{16,32},{32,48},{48,64},{64,80},{80,96},{96,112},{112,128},... | collective-permute-start | bytes 786440 | tf_op jit(solution)/shard_map/while/body/eval_jaxpr/ppermute | solution.py:12
  264.3 14.5 %all-to-all-start = ((bf16[16,2,32,128]{3,2,1,0:T(8,128)(2,1)}), bf16[16,2,32,128]{3,2,1,0:T(8,128)(2,1)S(1)}, u32[]{:S(2)}, u32[]{:S(2)}) async-start(bf16[16,2,32,128]{3,2,1,0:T(8,128)(2,1)} %broadcast_select_fusion.3), calls=%async_computation | async-start | bytes 524288 | tf_op jit(solution)/shard_map/while/body/eval_jaxpr/all_to_all | solution.py:78
  282.7 13.0 %collective-permute-start = (bf16[32,32,128]{2,1,0:T(8,128)(2,1)S(1)}, bf16[32,32,128]{2,1,0:T(8,128)(2,1)S(1)}, u32[]{:S(2)}, u32[]{:S(2)}) collective-permute-start(bf16[32,32,128]{2,1,0:T(8,128)(2,1)S(1)} %get-tuple-element.421), channel_id=1, source_target_pairs={{0,16},{16,32},{32,48},{48,64},{64,80},{80,96},{96,112},{112,128},... | collective-permute-start | bytes 786440 | tf_op jit(solution)/shard_map/while/body/eval_jaxpr/ppermute | solution.py:12
  298.4 14.5 %all-to-all-start = ((bf16[16,2,32,128]{3,2,1,0:T(8,128)(2,1)}), bf16[16,2,32,128]{3,2,1,0:T(8,128)(2,1)S(1)}, u32[]{:S(2)}, u32[]{:S(2)}) async-start(bf16[16,2,32,128]{3,2,1,0:T(8,128)(2,1)} %broadcast_select_fusion.3), calls=%async_computation | async-start | bytes 524288 | tf_op jit(solution)/shard_map/while/body/eval_jaxpr/all_to_all | solution.py:78
  316.7 13.0 %collective-permute-start = (bf16[32,32,128]{2,1,0:T(8,128)(2,1)S(1)}, bf16[32,32,128]{2,1,0:T(8,128)(2,1)S(1)}, u32[]{:S(2)}, u32[]{:S(2)}) collective-permute-start(bf16[32,32,128]{2,1,0:T(8,128)(2,1)S(1)} %get-tuple-element.421), channel_id=1, source_target_pairs={{0,16},{16,32},{32,48},{48,64},{64,80},{80,96},{96,112},{112,128},... | collective-permute-start | bytes 786440 | tf_op jit(solution)/shard_map/while/body/eval_jaxpr/ppermute | solution.py:12
  332.4 14.5 %all-to-all-start = ((bf16[16,2,32,128]{3,2,1,0:T(8,128)(2,1)}), bf16[16,2,32,128]{3,2,1,0:T(8,128)(2,1)S(1)}, u32[]{:S(2)}, u32[]{:S(2)}) async-start(bf16[16,2,32,128]{3,2,1,0:T(8,128)(2,1)} %broadcast_select_fusion.3), calls=%async_computation | async-start | bytes 524288 | tf_op jit(solution)/shard_map/while/body/eval_jaxpr/all_to_all | solution.py:78
  350.8 13.0 %collective-permute-start = (bf16[32,32,128]{2,1,0:T(8,128)(2,1)S(1)}, bf16[32,32,128]{2,1,0:T(8,128)(2,1)S(1)}, u32[]{:S(2)}, u32[]{:S(2)}) collective-permute-start(bf16[32,32,128]{2,1,0:T(8,128)(2,1)S(1)} %get-tuple-element.421), channel_id=1, source_target_pairs={{0,16},{16,32},{32,48},{48,64},{64,80},{80,96},{96,112},{112,128},... | collective-permute-start | bytes 786440 | tf_op jit(solution)/shard_map/while/body/eval_jaxpr/ppermute | solution.py:12
  366.4 14.5 %all-to-all-start = ((bf16[16,2,32,128]{3,2,1,0:T(8,128)(2,1)}), bf16[16,2,32,128]{3,2,1,0:T(8,128)(2,1)S(1)}, u32[]{:S(2)}, u32[]{:S(2)}) async-start(bf16[16,2,32,128]{3,2,1,0:T(8,128)(2,1)} %broadcast_select_fusion.3), calls=%async_computation | async-start | bytes 524288 | tf_op jit(solution)/shard_map/while/body/eval_jaxpr/all_to_all | solution.py:78
  384.8 13.0 %collective-permute-start = (bf16[32,32,128]{2,1,0:T(8,128)(2,1)S(1)}, bf16[32,32,128]{2,1,0:T(8,128)(2,1)S(1)}, u32[]{:S(2)}, u32[]{:S(2)}) collective-permute-start(bf16[32,32,128]{2,1,0:T(8,128)(2,1)S(1)} %get-tuple-element.421), channel_id=1, source_target_pairs={{0,16},{16,32},{32,48},{48,64},{64,80},{80,96},{96,112},{112,128},... | collective-permute-start | bytes 786440 | tf_op jit(solution)/shard_map/while/body/eval_jaxpr/ppermute | solution.py:12
  400.5 14.5 %all-to-all-start = ((bf16[16,2,32,128]{3,2,1,0:T(8,128)(2,1)}), bf16[16,2,32,128]{3,2,1,0:T(8,128)(2,1)S(1)}, u32[]{:S(2)}, u32[]{:S(2)}) async-start(bf16[16,2,32,128]{3,2,1,0:T(8,128)(2,1)} %broadcast_select_fusion.3), calls=%async_computation | async-start | bytes 524288 | tf_op jit(solution)/shard_map/while/body/eval_jaxpr/all_to_all | solution.py:78
  418.9 13.0 %collective-permute-start = (bf16[32,32,128]{2,1,0:T(8,128)(2,1)S(1)}, bf16[32,32,128]{2,1,0:T(8,128)(2,1)S(1)}, u32[]{:S(2)}, u32[]{:S(2)}) collective-permute-start(bf16[32,32,128]{2,1,0:T(8,128)(2,1)S(1)} %get-tuple-element.421), channel_id=1, source_target_pairs={{0,16},{16,32},{32,48},{48,64},{64,80},{80,96},{96,112},{112,128},... | collective-permute-start | bytes 786440 | tf_op jit(solution)/shard_map/while/body/eval_jaxpr/ppermute | solution.py:12
  434.5 14.5 %all-to-all-start = ((bf16[16,2,32,128]{3,2,1,0:T(8,128)(2,1)}), bf16[16,2,32,128]{3,2,1,0:T(8,128)(2,1)S(1)}, u32[]{:S(2)}, u32[]{:S(2)}) async-start(bf16[16,2,32,128]{3,2,1,0:T(8,128)(2,1)} %broadcast_select_fusion.3), calls=%async_computation | async-start | bytes 524288 | tf_op jit(solution)/shard_map/while/body/eval_jaxpr/all_to_all | solution.py:78
  452.9 13.0 %collective-permute-start = (bf16[32,32,128]{2,1,0:T(8,128)(2,1)S(1)}, bf16[32,32,128]{2,1,0:T(8,128)(2,1)S(1)}, u32[]{:S(2)}, u32[]{:S(2)}) collective-permute-start(bf16[32,32,128]{2,1,0:T(8,128)(2,1)S(1)} %get-tuple-element.421), channel_id=1, source_target_pairs={{0,16},{16,32},{32,48},{48,64},{64,80},{80,96},{96,112},{112,128},... | collective-permute-start | bytes 786440 | tf_op jit(solution)/shard_map/while/body/eval_jaxpr/ppermute | solution.py:12
  468.5 14.5 %all-to-all-start = ((bf16[16,2,32,128]{3,2,1,0:T(8,128)(2,1)}), bf16[16,2,32,128]{3,2,1,0:T(8,128)(2,1)S(1)}, u32[]{:S(2)}, u32[]{:S(2)}) async-start(bf16[16,2,32,128]{3,2,1,0:T(8,128)(2,1)} %broadcast_select_fusion.3), calls=%async_computation | async-start | bytes 524288 | tf_op jit(solution)/shard_map/while/body/eval_jaxpr/all_to_all | solution.py:78
  486.9 13.0 %collective-permute-start = (bf16[32,32,128]{2,1,0:T(8,128)(2,1)S(1)}, bf16[32,32,128]{2,1,0:T(8,128)(2,1)S(1)}, u32[]{:S(2)}, u32[]{:S(2)}) collective-permute-start(bf16[32,32,128]{2,1,0:T(8,128)(2,1)S(1)} %get-tuple-element.421), channel_id=1, source_target_pairs={{0,16},{16,32},{32,48},{48,64},{64,80},{80,96},{96,112},{112,128},... | collective-permute-start | bytes 786440 | tf_op jit(solution)/shard_map/while/body/eval_jaxpr/ppermute | solution.py:12
  502.6 14.5 %all-to-all-start = ((bf16[16,2,32,128]{3,2,1,0:T(8,128)(2,1)}), bf16[16,2,32,128]{3,2,1,0:T(8,128)(2,1)S(1)}, u32[]{:S(2)}, u32[]{:S(2)}) async-start(bf16[16,2,32,128]{3,2,1,0:T(8,128)(2,1)} %broadcast_select_fusion.3), calls=%async_computation | async-start | bytes 524288 | tf_op jit(solution)/shard_map/while/body/eval_jaxpr/all_to_all | solution.py:78
  521.0 13.0 %collective-permute-start = (bf16[32,32,128]{2,1,0:T(8,128)(2,1)S(1)}, bf16[32,32,128]{2,1,0:T(8,128)(2,1)S(1)}, u32[]{:S(2)}, u32[]{:S(2)}) collective-permute-start(bf16[32,32,128]{2,1,0:T(8,128)(2,1)S(1)} %get-tuple-element.421), channel_id=1, source_target_pairs={{0,16},{16,32},{32,48},{48,64},{64,80},{80,96},{96,112},{112,128},... | collective-permute-start | bytes 786440 | tf_op jit(solution)/shard_map/while/body/eval_jaxpr/ppermute | solution.py:12
  536.6 14.5 %all-to-all-start = ((bf16[16,2,32,128]{3,2,1,0:T(8,128)(2,1)}), bf16[16,2,32,128]{3,2,1,0:T(8,128)(2,1)S(1)}, u32[]{:S(2)}, u32[]{:S(2)}) async-start(bf16[16,2,32,128]{3,2,1,0:T(8,128)(2,1)} %broadcast_select_fusion.3), calls=%async_computation | async-start | bytes 524288 | tf_op jit(solution)/shard_map/while/body/eval_jaxpr/all_to_all | solution.py:78
  570.7 14.5 %all-to-all-start = ((bf16[16,2,32,128]{3,2,1,0:T(8,128)(2,1)}), bf16[16,2,32,128]{3,2,1,0:T(8,128)(2,1)S(1)}, u32[]{:S(2)}, u32[]{:S(2)}) async-start(bf16[16,2,32,128]{3,2,1,0:T(8,128)(2,1)} %broadcast_select_fusion.3), calls=%async_computation | async-start | bytes 524288 | tf_op jit(solution)/shard_map/while/body/eval_jaxpr/all_to_all | solution.py:78
  589.0 13.0 %collective-permute-start = (bf16[32,32,128]{2,1,0:T(8,128)(2,1)S(1)}, bf16[32,32,128]{2,1,0:T(8,128)(2,1)S(1)}, u32[]{:S(2)}, u32[]{:S(2)}) collective-permute-start(bf16[32,32,128]{2,1,0:T(8,128)(2,1)S(1)} %get-tuple-element.421), channel_id=1, source_target_pairs={{0,16},{16,32},{32,48},{48,64},{64,80},{80,96},{96,112},{112,128},... | collective-permute-start | bytes 786440 | tf_op jit(solution)/shard_map/while/body/eval_jaxpr/ppermute | solution.py:12
  604.7 14.5 %all-to-all-start = ((bf16[16,2,32,128]{3,2,1,0:T(8,128)(2,1)}), bf16[16,2,32,128]{3,2,1,0:T(8,128)(2,1)S(1)}, u32[]{:S(2)}, u32[]{:S(2)}) async-start(bf16[16,2,32,128]{3,2,1,0:T(8,128)(2,1)} %broadcast_select_fusion.3), calls=%async_computation | async-start | bytes 524288 | tf_op jit(solution)/shard_map/while/body/eval_jaxpr/all_to_all | solution.py:78
  623.1 13.0 %collective-permute-start = (bf16[32,32,128]{2,1,0:T(8,128)(2,1)S(1)}, bf16[32,32,128]{2,1,0:T(8,128)(2,1)S(1)}, u32[]{:S(2)}, u32[]{:S(2)}) collective-permute-start(bf16[32,32,128]{2,1,0:T(8,128)(2,1)S(1)} %get-tuple-element.421), channel_id=1, source_target_pairs={{0,16},{16,32},{32,48},{48,64},{64,80},{80,96},{96,112},{112,128},... | collective-permute-start | bytes 786440 | tf_op jit(solution)/shard_map/while/body/eval_jaxpr/ppermute | solution.py:12
  638.7 14.5 %all-to-all-start = ((bf16[16,2,32,128]{3,2,1,0:T(8,128)(2,1)}), bf16[16,2,32,128]{3,2,1,0:T(8,128)(2,1)S(1)}, u32[]{:S(2)}, u32[]{:S(2)}) async-start(bf16[16,2,32,128]{3,2,1,0:T(8,128)(2,1)} %broadcast_select_fusion.3), calls=%async_computation | async-start | bytes 524288 | tf_op jit(solution)/shard_map/while/body/eval_jaxpr/all_to_all | solution.py:78
  672.8 14.5 %all-to-all-start = ((bf16[16,2,32,128]{3,2,1,0:T(8,128)(2,1)}), bf16[16,2,32,128]{3,2,1,0:T(8,128)(2,1)S(1)}, u32[]{:S(2)}, u32[]{:S(2)}) async-start(bf16[16,2,32,128]{3,2,1,0:T(8,128)(2,1)} %broadcast_select_fusion.3), calls=%async_computation | async-start | bytes 524288 | tf_op jit(solution)/shard_map/while/body/eval_jaxpr/all_to_all | solution.py:78
  707.0 31.1 %all-to-all-start.1 = ((bf16[4,16,2,4096]{3,2,0,1:T(2,128)(2,1)}), bf16[4,16,2,4096]{3,2,0,1:T(2,128)(2,1)S(1)}, u32[]{:S(2)}, u32[]{:S(2)}) async-start(bf16[4,16,2,4096]{3,2,0,1:T(2,128)(2,1)} %copy.26), calls=%async_computation.1 | async-start | bytes 2097152 | tf_op jit(solution)/shard_map/all_to_all | solution.py:107
  (10 other events, 168.4 us)
Sparse Core Ops, SparseCore 0:
  9.8 50.1 all-gather.2
where the time goes:
time: 750 us; the launch traced here: 746 us
  waiting for transfers between devices  371 us (49%)
  starting transfers between devices  194 us (26%)
  local copies, waits for them, and re-layouts  59.3 us (8%)
  matrix products  58.6 us (8%)
  other arithmetic  25.8 us (3%)
  blocking collectives  20.7 us (3%)
  between operations  13.5 us (2%)
    all_to_all x19, waiting for transfers between devices, apply_layer(): lax.all_to_all(payload, 'col', split_axis=0, concat_axis=0, tiled=True)  206 us
    ppermute x19, waiting for transfers between devices, from_behind(): return lax.ppermute(x, axis, pairs)  128 us
    ppermute x19, starting transfers between devices, from_behind(): return lax.ppermute(x, axis, pairs)  109 us
    all_to_all x19, starting transfers between devices, apply_layer(): lax.all_to_all(payload, 'col', split_axis=0, concat_axis=0, tiled=True)  70.7 us
    dot_general x19, matrix products, combine(): jnp.einsum('ckrb,ckbo->cro', picked, local_w, preferred_element_type=jnp....  58.6 us
    all_gather x1, waiting for transfers between devices, body(): all_inputs = lax.all_gather(features, 'section', axis=1, tiled=True)  21.1 us
    all_gather x1, blocking collectives, body(): pattern_table = lax.all_gather(sources[0], 'col', axis=0, tiled=True)  20.7 us
    dynamic_slice x19, local copies, waits for them, and re-layouts, tick(): lax.dynamic_index_in_dim(blocks_in, jnp.minimum(tick_idx, piece_total - 1...  18.6 us
  transfers between devices with their start and end apart: 40, of which 40 were waited for; matrix products, arithmetic and copies ran while one was open for 2% of the time, Pallas kernels for 0%

commit v1 on v0

--- a/solution.py
+++ b/solution.py
@@ -38,7 +38,21 @@
     block_size = local_w.shape[2]
     local_src = sources[0].reshape(blocks_own * nonzero_count)
     local_bias = bias[0].reshape(blocks_own, 1, block_size)
-    pattern_table = lax.all_gather(sources[0], "col", axis=0, tiled=True)
+    ways, here, step = (lax.axis_size("col"), lax.axis_index("col"), sources[0].shape[0])
+    shape = [n * ways if d == 0 else n for d, n in enumerate(sources[0].shape)]
+    full = lax.dynamic_update_slice_in_dim(
+        jnp.zeros(shape, sources[0].dtype), sources[0], here * step, axis=0
+    )
+    going_up = going_down = sources[0]
+    for far in range(1, ways // 2 + 1):
+        going_up = lax.ppermute(going_up, "col", [(d, (d + 1) % ways) for d in range(ways)])
+        full = lax.dynamic_update_slice_in_dim(full, going_up, (here - far) % ways * step, axis=0)
+        if 2 * far < ways:
+            going_down = lax.ppermute(going_down, "col", [(d, (d - 1) % ways) for d in range(ways)])
+            full = lax.dynamic_update_slice_in_dim(
+                full, going_down, (here + far) % ways * step, axis=0
+            )
+    pattern_table = full
     positions, present = request_lists(pattern_table, owners, blocks_own, CAP)
     outgoing = lax.dynamic_index_in_dim(positions, col_idx, 1, keepdims=False).reshape(owners * CAP)
     incoming = lax.dynamic_index_in_dim(positions, col_idx, 0, keepdims=False)

time: 750 us -> 749 us (level)
  starting transfers between devices: 194 us -> 217 us
  blocking collectives: 20.7 us -> 0 us
    ppermute x0 -> x15, starting transfers between devices: none -> 23.2 us  [the longest x7 23.1 us: body(): lax.ppermute(going_down, 'col', [(d, (d - 1) % ways) for d in range(ways)])]
    all_gather x1 -> x0, blocking collectives: 20.7 us -> none  [body(): pattern_table = lax.all_gather(sources[0], 'col', axis=0, tiled=True)]
    all_gather x1, waiting for transfers between devices: 21.1 us -> 7.39 us  [body(): all_inputs = lax.all_gather(features, 'section', axis=1, tiled=True)]
    ppermute x0 -> x15, waiting for transfers between devices: none -> 11.3 us  [the longest x8 10.2 us: body(): lax.ppermute(going_up, 'col', [(d, (d + 1) % ways) for d in range(ways)])]
  transfers between devices with their start and end apart: 40 -> 55, of which waited for: 40 -> 51; matrix products, arithmetic and copies ran while one was open for 2% -> 2% of each run, Pallas kernels for 0% -> 0%
where the time goes in v1:
time: 749 us; the launch traced here: 745 us
  waiting for transfers between devices  369 us (49%)
  starting transfers between devices  217 us (29%)
  local copies, waits for them, and re-layouts  60 us (8%)
  matrix products  58.6 us (8%)
  other arithmetic  24.3 us (3%)
  between operations  13.9 us (2%)
    all_to_all x19, waiting for transfers between devices, apply_layer(): lax.all_to_all(payload, 'col', split_axis=0, concat_axis=0, tiled=True)  206 us
    ppermute x19, waiting for transfers between devices, from_behind(): return lax.ppermute(x, axis, pairs)  128 us
    ppermute x19, starting transfers between devices, from_behind(): return lax.ppermute(x, axis, pairs)  109 us
    all_to_all x19, starting transfers between devices, apply_layer(): lax.all_to_all(payload, 'col', split_axis=0, concat_axis=0, tiled=True)  70.6 us
    dot_general x19, matrix products, combine(): jnp.einsum('ckrb,ckbo->cro', picked, local_w, preferred_element_type=jnp....  58.6 us
    ppermute x7, starting transfers between devices, body(): lax.ppermute(going_down, 'col', [(d, (d - 1) % ways) for d in range(ways)])  23.1 us
    dynamic_slice x19, local copies, waits for them, and re-layouts, tick(): lax.dynamic_index_in_dim(blocks_in, jnp.minimum(tick_idx, piece_total - 1...  18.6 us
    all_to_all x1, waiting for transfers between devices, body(): lax.all_to_all(outgoing_rows, 'section', split_axis=1, concat_axis=1, til...  16.6 us
  transfers between devices with their start and end apart: 55, of which 51 were waited for; matrix products, arithmetic and copies ran while one was open for 2% of the time, Pallas kernels for 0%

profile of v1, /device:TPU:8, one launch (start us, length us, event | category | flops | bytes accessed | tf_op | source)
XLA Modules:
  0.0 745.4 jit_solution(12340416438863014826)
XLA Ops:
  52.6 7.4 all-gather.2.cloned.1.call-done
  63.1 640.8 %while.19 = (s32[]{:T(128)}, bf16[32,32,128]{2,1,0:T(8,128)(2,1)S(1)}, bf16[4,32,32,128]{3,2,1,0:T(8,128)(2,1)S(1)}, s32[128]{0:T(128)S(1)}, s32[32]{0:T(128)S(1...) while((s32[]{:T(128)}, ...), condition=%wide.region_6.7_spmd, body=%wide.region_5.6_spmd.sunk | while | flops 135531952 | bytes 12878729 | solution.py:114
  65.8 7.1 all-to-all-start
  73.1 11.0 %all-to-all-done = bf16[16,2,32,128]{3,2,1,0:T(8,128)(2,1)S(1)} async-done(((bf16[16,2,32,128]{3,2,1,0:T(8,128)(2,1)}), bf16[16,2,32,128]{3,2,1,0:T(8,128)(2,1)S(1)}, u32[]{:S(2)}, u32[]{:S(2)}) %all-to-all-start) | async-done | bytes 262176 | tf_op jit(solution)/shard_map/while/body/eval_jaxpr/all_to_all | solution.py:92
  91.1 7.8 %collective-permute-done = bf16[32,32,128]{2,1,0:T(8,128)(2,1)S(1)} collective-permute-done((bf16[32,32,128]{2,1,0:T(8,128)(2,1)S(1)}, bf16[32,32,128]{2,1,0:T(8,128)(2,1)S(1)}, u32[]{:S(2)}, u32[]{:S(2)}) %collective-permute-start) | collective-permute-done | bytes 262176 | tf_op jit(solution)/shard_map/while/body/eval_jaxpr/ppermute | solution.py:12
  105.3 10.8 %all-to-all-done = bf16[16,2,32,128]{3,2,1,0:T(8,128)(2,1)S(1)} async-done(((bf16[16,2,32,128]{3,2,1,0:T(8,128)(2,1)}), bf16[16,2,32,128]{3,2,1,0:T(8,128)(2,1)S(1)}, u32[]{:S(2)}, u32[]{:S(2)}) %all-to-all-start) | async-done | bytes 262176 | tf_op jit(solution)/shard_map/while/body/eval_jaxpr/all_to_all | solution.py:92
  123.2 7.7 %collective-permute-done = bf16[32,32,128]{2,1,0:T(8,128)(2,1)S(1)} collective-permute-done((bf16[32,32,128]{2,1,0:T(8,128)(2,1)S(1)}, bf16[32,32,128]{2,1,0:T(8,128)(2,1)S(1)}, u32[]{:S(2)}, u32[]{:S(2)}) %collective-permute-start) | collective-permute-done | bytes 262176 | tf_op jit(solution)/shard_map/while/body/eval_jaxpr/ppermute | solution.py:12
  137.2 10.8 %all-to-all-done = bf16[16,2,32,128]{3,2,1,0:T(8,128)(2,1)S(1)} async-done(((bf16[16,2,32,128]{3,2,1,0:T(8,128)(2,1)}), bf16[16,2,32,128]{3,2,1,0:T(8,128)(2,1)S(1)}, u32[]{:S(2)}, u32[]{:S(2)}) %all-to-all-start) | async-done | bytes 262176 | tf_op jit(solution)/shard_map/while/body/eval_jaxpr/all_to_all | solution.py:92
  155.1 7.7 %collective-permute-done = bf16[32,32,128]{2,1,0:T(8,128)(2,1)S(1)} collective-permute-done((bf16[32,32,128]{2,1,0:T(8,128)(2,1)S(1)}, bf16[32,32,128]{2,1,0:T(8,128)(2,1)S(1)}, u32[]{:S(2)}, u32[]{:S(2)}) %collective-permute-start) | collective-permute-done | bytes 262176 | tf_op jit(solution)/shard_map/while/body/eval_jaxpr/ppermute | solution.py:12
  169.1 10.8 %all-to-all-done = bf16[16,2,32,128]{3,2,1,0:T(8,128)(2,1)S(1)} async-done(((bf16[16,2,32,128]{3,2,1,0:T(8,128)(2,1)}), bf16[16,2,32,128]{3,2,1,0:T(8,128)(2,1)S(1)}, u32[]{:S(2)}, u32[]{:S(2)}) %all-to-all-start) | async-done | bytes 262176 | tf_op jit(solution)/shard_map/while/body/eval_jaxpr/all_to_all | solution.py:92
  187.0 7.6 %collective-permute-done = bf16[32,32,128]{2,1,0:T(8,128)(2,1)S(1)} collective-permute-done((bf16[32,32,128]{2,1,0:T(8,128)(2,1)S(1)}, bf16[32,32,128]{2,1,0:T(8,128)(2,1)S(1)}, u32[]{:S(2)}, u32[]{:S(2)}) %collective-permute-start) | collective-permute-done | bytes 262176 | tf_op jit(solution)/shard_map/while/body/eval_jaxpr/ppermute | solution.py:12
  201.1 10.8 %all-to-all-done = bf16[16,2,32,128]{3,2,1,0:T(8,128)(2,1)S(1)} async-done(((bf16[16,2,32,128]{3,2,1,0:T(8,128)(2,1)}), bf16[16,2,32,128]{3,2,1,0:T(8,128)(2,1)S(1)}, u32[]{:S(2)}, u32[]{:S(2)}) %all-to-all-start) | async-done | bytes 262176 | tf_op jit(solution)/shard_map/while/body/eval_jaxpr/all_to_all | solution.py:92
  233.9 10.8 %all-to-all-done = bf16[16,2,32,128]{3,2,1,0:T(8,128)(2,1)S(1)} async-done(((bf16[16,2,32,128]{3,2,1,0:T(8,128)(2,1)}), bf16[16,2,32,128]{3,2,1,0:T(8,128)(2,1)S(1)}, u32[]{:S(2)}, u32[]{:S(2)}) %all-to-all-start) | async-done | bytes 262176 | tf_op jit(solution)/shard_map/while/body/eval_jaxpr/all_to_all | solution.py:92
  248.5 6.5 collective-permute-start
  267.9 10.8 %all-to-all-done = bf16[16,2,32,128]{3,2,1,0:T(8,128)(2,1)S(1)} async-done(((bf16[16,2,32,128]{3,2,1,0:T(8,128)(2,1)}), bf16[16,2,32,128]{3,2,1,0:T(8,128)(2,1)S(1)}, u32[]{:S(2)}, u32[]{:S(2)}) %all-to-all-start) | async-done | bytes 262176 | tf_op jit(solution)/shard_map/while/body/eval_jaxpr/all_to_all | solution.py:92
  282.6 6.5 collective-permute-start
  301.9 10.8 %all-to-all-done = bf16[16,2,32,128]{3,2,1,0:T(8,128)(2,1)S(1)} async-done(((bf16[16,2,32,128]{3,2,1,0:T(8,128)(2,1)}), bf16[16,2,32,128]{3,2,1,0:T(8,128)(2,1)S(1)}, u32[]{:S(2)}, u32[]{:S(2)}) %all-to-all-start) | async-done | bytes 262176 | tf_op jit(solution)/shard_map/while/body/eval_jaxpr/all_to_all | solution.py:92
  316.6 6.5 collective-permute-start
  336.0 10.8 %all-to-all-done = bf16[16,2,32,128]{3,2,1,0:T(8,128)(2,1)S(1)} async-done(((bf16[16,2,32,128]{3,2,1,0:T(8,128)(2,1)}), bf16[16,2,32,128]{3,2,1,0:T(8,128)(2,1)S(1)}, u32[]{:S(2)}, u32[]{:S(2)}) %all-to-all-start) | async-done | bytes 262176 | tf_op jit(solution)/shard_map/while/body/eval_jaxpr/all_to_all | solution.py:92
  350.6 6.5 collective-permute-start
  370.0 10.8 %all-to-all-done = bf16[16,2,32,128]{3,2,1,0:T(8,128)(2,1)S(1)} async-done(((bf16[16,2,32,128]{3,2,1,0:T(8,128)(2,1)}), bf16[16,2,32,128]{3,2,1,0:T(8,128)(2,1)S(1)}, u32[]{:S(2)}, u32[]{:S(2)}) %all-to-all-start) | async-done | bytes 262176 | tf_op jit(solution)/shard_map/while/body/eval_jaxpr/all_to_all | solution.py:92
  404.0 10.8 %all-to-all-done = bf16[16,2,32,128]{3,2,1,0:T(8,128)(2,1)S(1)} async-done(((bf16[16,2,32,128]{3,2,1,0:T(8,128)(2,1)}), bf16[16,2,32,128]{3,2,1,0:T(8,128)(2,1)S(1)}, u32[]{:S(2)}, u32[]{:S(2)}) %all-to-all-start) | async-done | bytes 262176 | tf_op jit(solution)/shard_map/while/body/eval_jaxpr/all_to_all | solution.py:92
  438.0 10.8 %all-to-all-done = bf16[16,2,32,128]{3,2,1,0:T(8,128)(2,1)S(1)} async-done(((bf16[16,2,32,128]{3,2,1,0:T(8,128)(2,1)}), bf16[16,2,32,128]{3,2,1,0:T(8,128)(2,1)S(1)}, u32[]{:S(2)}, u32[]{:S(2)}) %all-to-all-start) | async-done | bytes 262176 | tf_op jit(solution)/shard_map/while/body/eval_jaxpr/all_to_all | solution.py:92
  472.1 10.8 %all-to-all-done = bf16[16,2,32,128]{3,2,1,0:T(8,128)(2,1)S(1)} async-done(((bf16[16,2,32,128]{3,2,1,0:T(8,128)(2,1)}), bf16[16,2,32,128]{3,2,1,0:T(8,128)(2,1)S(1)}, u32[]{:S(2)}, u32[]{:S(2)}) %all-to-all-start) | async-done | bytes 262176 | tf_op jit(solution)/shard_map/while/body/eval_jaxpr/all_to_all | solution.py:92
  506.1 10.8 %all-to-all-done = bf16[16,2,32,128]{3,2,1,0:T(8,128)(2,1)S(1)} async-done(((bf16[16,2,32,128]{3,2,1,0:T(8,128)(2,1)}), bf16[16,2,32,128]{3,2,1,0:T(8,128)(2,1)S(1)}, u32[]{:S(2)}, u32[]{:S(2)}) %all-to-all-start) | async-done | bytes 262176 | tf_op jit(solution)/shard_map/while/body/eval_jaxpr/all_to_all | solution.py:92
  540.1 10.8 %all-to-all-done = bf16[16,2,32,128]{3,2,1,0:T(8,128)(2,1)S(1)} async-done(((bf16[16,2,32,128]{3,2,1,0:T(8,128)(2,1)}), bf16[16,2,32,128]{3,2,1,0:T(8,128)(2,1)S(1)}, u32[]{:S(2)}, u32[]{:S(2)}) %all-to-all-start) | async-done | bytes 262176 | tf_op jit(solution)/shard_map/while/body/eval_jaxpr/all_to_all | solution.py:92
  574.2 10.8 %all-to-all-done = bf16[16,2,32,128]{3,2,1,0:T(8,128)(2,1)S(1)} async-done(((bf16[16,2,32,128]{3,2,1,0:T(8,128)(2,1)}), bf16[16,2,32,128]{3,2,1,0:T(8,128)(2,1)S(1)}, u32[]{:S(2)}, u32[]{:S(2)}) %all-to-all-start) | async-done | bytes 262176 | tf_op jit(solution)/shard_map/while/body/eval_jaxpr/all_to_all | solution.py:92
  608.2 10.8 %all-to-all-done = bf16[16,2,32,128]{3,2,1,0:T(8,128)(2,1)S(1)} async-done(((bf16[16,2,32,128]{3,2,1,0:T(8,128)(2,1)}), bf16[16,2,32,128]{3,2,1,0:T(8,128)(2,1)S(1)}, u32[]{:S(2)}, u32[]{:S(2)}) %all-to-all-start) | async-done | bytes 262176 | tf_op jit(solution)/shard_map/while/body/eval_jaxpr/all_to_all | solution.py:92
  642.2 10.8 %all-to-all-done = bf16[16,2,32,128]{3,2,1,0:T(8,128)(2,1)S(1)} async-done(((bf16[16,2,32,128]{3,2,1,0:T(8,128)(2,1)}), bf16[16,2,32,128]{3,2,1,0:T(8,128)(2,1)S(1)}, u32[]{:S(2)}, u32[]{:S(2)}) %all-to-all-start) | async-done | bytes 262176 | tf_op jit(solution)/shard_map/while/body/eval_jaxpr/all_to_all | solution.py:92
  676.2 10.8 %all-to-all-done = bf16[16,2,32,128]{3,2,1,0:T(8,128)(2,1)S(1)} async-done(((bf16[16,2,32,128]{3,2,1,0:T(8,128)(2,1)}), bf16[16,2,32,128]{3,2,1,0:T(8,128)(2,1)S(1)}, u32[]{:S(2)}, u32[]{:S(2)}) %all-to-all-start) | async-done | bytes 262176 | tf_op jit(solution)/shard_map/while/body/eval_jaxpr/all_to_all | solution.py:92
  706.8 14.3 %all-to-all-start.1 = ((bf16[4,16,2,4096]{3,2,0,1:T(2,128)(2,1)}), bf16[4,16,2,4096]{3,2,0,1:T(2,128)(2,1)S(1)}, u32[]{:S(2)}, u32[]{:S(2)}) async-start(bf16[4,16,2,4096]{3,2,0,1:T(2,128)(2,1)} %copy.71), calls=%async_computation.1 | async-start | bytes 2097152 | tf_op jit(solution)/shard_map/all_to_all | solution.py:121
  721.2 16.6 %all-to-all-done.1 = bf16[4,16,2,4096]{3,2,0,1:T(2,128)(2,1)S(1)} async-done(((bf16[4,16,2,4096]{3,2,0,1:T(2,128)(2,1)}), bf16[4,16,2,4096]{3,2,0,1:T(2,128)(2,1)S(1)}, u32[]{:S(2)}, u32[]{:S(2)}) %all-to-all-start.1) | async-done | bytes 1048608 | tf_op jit(solution)/shard_map/all_to_all | solution.py:121
  (435 shorter events, 421.6 us)
Async XLA Ops:
  6.5 53.5 %all-gather.2.cloned.1.call-start = ((), (), s32[]{:S(2)}) async-start(), calls=%async_computation.2 | async-start | bytes 1114112 | tf_op jit(solution)/shard_map/all_gather | solution.py:67
  65.8 18.3 %all-to-all-start = ((bf16[16,2,32,128]{3,2,1,0:T(8,128)(2,1)}), bf16[16,2,32,128]{3,2,1,0:T(8,128)(2,1)S(1)}, u32[]{:S(2)}, u32[]{:S(2)}) async-start(bf16[16,2,32,128]{3,2,1,0:T(8,128)(2,1)} %broadcast_select_fusion.3), calls=%async_computation | async-start | bytes 524288 | tf_op jit(solution)/shard_map/while/body/eval_jaxpr/all_to_all | solution.py:92
  101.6 14.5 %all-to-all-start = ((bf16[16,2,32,128]{3,2,1,0:T(8,128)(2,1)}), bf16[16,2,32,128]{3,2,1,0:T(8,128)(2,1)S(1)}, u32[]{:S(2)}, u32[]{:S(2)}) async-start(bf16[16,2,32,128]{3,2,1,0:T(8,128)(2,1)} %broadcast_select_fusion.3), calls=%async_computation | async-start | bytes 524288 | tf_op jit(solution)/shard_map/while/body/eval_jaxpr/all_to_all | solution.py:92
  133.5 14.5 %all-to-all-start = ((bf16[16,2,32,128]{3,2,1,0:T(8,128)(2,1)}), bf16[16,2,32,128]{3,2,1,0:T(8,128)(2,1)S(1)}, u32[]{:S(2)}, u32[]{:S(2)}) async-start(bf16[16,2,32,128]{3,2,1,0:T(8,128)(2,1)} %broadcast_select_fusion.3), calls=%async_computation | async-start | bytes 524288 | tf_op jit(solution)/shard_map/while/body/eval_jaxpr/all_to_all | solution.py:92
  165.4 14.5 %all-to-all-start = ((bf16[16,2,32,128]{3,2,1,0:T(8,128)(2,1)}), bf16[16,2,32,128]{3,2,1,0:T(8,128)(2,1)S(1)}, u32[]{:S(2)}, u32[]{:S(2)}) async-start(bf16[16,2,32,128]{3,2,1,0:T(8,128)(2,1)} %broadcast_select_fusion.3), calls=%async_computation | async-start | bytes 524288 | tf_op jit(solution)/shard_map/while/body/eval_jaxpr/all_to_all | solution.py:92
  197.3 14.5 %all-to-all-start = ((bf16[16,2,32,128]{3,2,1,0:T(8,128)(2,1)}), bf16[16,2,32,128]{3,2,1,0:T(8,128)(2,1)S(1)}, u32[]{:S(2)}, u32[]{:S(2)}) async-start(bf16[16,2,32,128]{3,2,1,0:T(8,128)(2,1)} %broadcast_select_fusion.3), calls=%async_computation | async-start | bytes 524288 | tf_op jit(solution)/shard_map/while/body/eval_jaxpr/all_to_all | solution.py:92
  230.1 14.5 %all-to-all-start = ((bf16[16,2,32,128]{3,2,1,0:T(8,128)(2,1)}), bf16[16,2,32,128]{3,2,1,0:T(8,128)(2,1)S(1)}, u32[]{:S(2)}, u32[]{:S(2)}) async-start(bf16[16,2,32,128]{3,2,1,0:T(8,128)(2,1)} %broadcast_select_fusion.3), calls=%async_computation | async-start | bytes 524288 | tf_op jit(solution)/shard_map/while/body/eval_jaxpr/all_to_all | solution.py:92
  248.5 13.0 %collective-permute-start = (bf16[32,32,128]{2,1,0:T(8,128)(2,1)S(1)}, bf16[32,32,128]{2,1,0:T(8,128)(2,1)S(1)}, u32[]{:S(2)}, u32[]{:S(2)}) collective-permute-start(bf16[32,32,128]{2,1,0:T(8,128)(2,1)S(1)} %get-tuple-element.421), channel_id=1, source_target_pairs={{0,16},{16,32},{32,48},{48,64},{64,80},{80,96},{96,112},{112,128},... | collective-permute-start | bytes 786440 | tf_op jit(solution)/shard_map/while/body/eval_jaxpr/ppermute | solution.py:12
  264.2 14.5 %all-to-all-start = ((bf16[16,2,32,128]{3,2,1,0:T(8,128)(2,1)}), bf16[16,2,32,128]{3,2,1,0:T(8,128)(2,1)S(1)}, u32[]{:S(2)}, u32[]{:S(2)}) async-start(bf16[16,2,32,128]{3,2,1,0:T(8,128)(2,1)} %broadcast_select_fusion.3), calls=%async_computation | async-start | bytes 524288 | tf_op jit(solution)/shard_map/while/body/eval_jaxpr/all_to_all | solution.py:92
  282.6 13.0 %collective-permute-start = (bf16[32,32,128]{2,1,0:T(8,128)(2,1)S(1)}, bf16[32,32,128]{2,1,0:T(8,128)(2,1)S(1)}, u32[]{:S(2)}, u32[]{:S(2)}) collective-permute-start(bf16[32,32,128]{2,1,0:T(8,128)(2,1)S(1)} %get-tuple-element.421), channel_id=1, source_target_pairs={{0,16},{16,32},{32,48},{48,64},{64,80},{80,96},{96,112},{112,128},... | collective-permute-start | bytes 786440 | tf_op jit(solution)/shard_map/while/body/eval_jaxpr/ppermute | solution.py:12
  298.2 14.5 %all-to-all-start = ((bf16[16,2,32,128]{3,2,1,0:T(8,128)(2,1)}), bf16[16,2,32,128]{3,2,1,0:T(8,128)(2,1)S(1)}, u32[]{:S(2)}, u32[]{:S(2)}) async-start(bf16[16,2,32,128]{3,2,1,0:T(8,128)(2,1)} %broadcast_select_fusion.3), calls=%async_computation | async-start | bytes 524288 | tf_op jit(solution)/shard_map/while/body/eval_jaxpr/all_to_all | solution.py:92
  316.6 13.0 %collective-permute-start = (bf16[32,32,128]{2,1,0:T(8,128)(2,1)S(1)}, bf16[32,32,128]{2,1,0:T(8,128)(2,1)S(1)}, u32[]{:S(2)}, u32[]{:S(2)}) collective-permute-start(bf16[32,32,128]{2,1,0:T(8,128)(2,1)S(1)} %get-tuple-element.421), channel_id=1, source_target_pairs={{0,16},{16,32},{32,48},{48,64},{64,80},{80,96},{96,112},{112,128},... | collective-permute-start | bytes 786440 | tf_op jit(solution)/shard_map/while/body/eval_jaxpr/ppermute | solution.py:12
  332.2 14.5 %all-to-all-start = ((bf16[16,2,32,128]{3,2,1,0:T(8,128)(2,1)}), bf16[16,2,32,128]{3,2,1,0:T(8,128)(2,1)S(1)}, u32[]{:S(2)}, u32[]{:S(2)}) async-start(bf16[16,2,32,128]{3,2,1,0:T(8,128)(2,1)} %broadcast_select_fusion.3), calls=%async_computation | async-start | bytes 524288 | tf_op jit(solution)/shard_map/while/body/eval_jaxpr/all_to_all | solution.py:92
  350.6 13.0 %collective-permute-start = (bf16[32,32,128]{2,1,0:T(8,128)(2,1)S(1)}, bf16[32,32,128]{2,1,0:T(8,128)(2,1)S(1)}, u32[]{:S(2)}, u32[]{:S(2)}) collective-permute-start(bf16[32,32,128]{2,1,0:T(8,128)(2,1)S(1)} %get-tuple-element.421), channel_id=1, source_target_pairs={{0,16},{16,32},{32,48},{48,64},{64,80},{80,96},{96,112},{112,128},... | collective-permute-start | bytes 786440 | tf_op jit(solution)/shard_map/while/body/eval_jaxpr/ppermute | solution.py:12
  366.3 14.5 %all-to-all-start = ((bf16[16,2,32,128]{3,2,1,0:T(8,128)(2,1)}), bf16[16,2,32,128]{3,2,1,0:T(8,128)(2,1)S(1)}, u32[]{:S(2)}, u32[]{:S(2)}) async-start(bf16[16,2,32,128]{3,2,1,0:T(8,128)(2,1)} %broadcast_select_fusion.3), calls=%async_computation | async-start | bytes 524288 | tf_op jit(solution)/shard_map/while/body/eval_jaxpr/all_to_all | solution.py:92
  384.6 13.0 %collective-permute-start = (bf16[32,32,128]{2,1,0:T(8,128)(2,1)S(1)}, bf16[32,32,128]{2,1,0:T(8,128)(2,1)S(1)}, u32[]{:S(2)}, u32[]{:S(2)}) collective-permute-start(bf16[32,32,128]{2,1,0:T(8,128)(2,1)S(1)} %get-tuple-element.421), channel_id=1, source_target_pairs={{0,16},{16,32},{32,48},{48,64},{64,80},{80,96},{96,112},{112,128},... | collective-permute-start | bytes 786440 | tf_op jit(solution)/shard_map/while/body/eval_jaxpr/ppermute | solution.py:12
  400.3 14.5 %all-to-all-start = ((bf16[16,2,32,128]{3,2,1,0:T(8,128)(2,1)}), bf16[16,2,32,128]{3,2,1,0:T(8,128)(2,1)S(1)}, u32[]{:S(2)}, u32[]{:S(2)}) async-start(bf16[16,2,32,128]{3,2,1,0:T(8,128)(2,1)} %broadcast_select_fusion.3), calls=%async_computation | async-start | bytes 524288 | tf_op jit(solution)/shard_map/while/body/eval_jaxpr/all_to_all | solution.py:92
  418.7 13.0 %collective-permute-start = (bf16[32,32,128]{2,1,0:T(8,128)(2,1)S(1)}, bf16[32,32,128]{2,1,0:T(8,128)(2,1)S(1)}, u32[]{:S(2)}, u32[]{:S(2)}) collective-permute-start(bf16[32,32,128]{2,1,0:T(8,128)(2,1)S(1)} %get-tuple-element.421), channel_id=1, source_target_pairs={{0,16},{16,32},{32,48},{48,64},{64,80},{80,96},{96,112},{112,128},... | collective-permute-start | bytes 786440 | tf_op jit(solution)/shard_map/while/body/eval_jaxpr/ppermute | solution.py:12
  434.3 14.5 %all-to-all-start = ((bf16[16,2,32,128]{3,2,1,0:T(8,128)(2,1)}), bf16[16,2,32,128]{3,2,1,0:T(8,128)(2,1)S(1)}, u32[]{:S(2)}, u32[]{:S(2)}) async-start(bf16[16,2,32,128]{3,2,1,0:T(8,128)(2,1)} %broadcast_select_fusion.3), calls=%async_computation | async-start | bytes 524288 | tf_op jit(solution)/shard_map/while/body/eval_jaxpr/all_to_all | solution.py:92
  452.7 13.0 %collective-permute-start = (bf16[32,32,128]{2,1,0:T(8,128)(2,1)S(1)}, bf16[32,32,128]{2,1,0:T(8,128)(2,1)S(1)}, u32[]{:S(2)}, u32[]{:S(2)}) collective-permute-start(bf16[32,32,128]{2,1,0:T(8,128)(2,1)S(1)} %get-tuple-element.421), channel_id=1, source_target_pairs={{0,16},{16,32},{32,48},{48,64},{64,80},{80,96},{96,112},{112,128},... | collective-permute-start | bytes 786440 | tf_op jit(solution)/shard_map/while/body/eval_jaxpr/ppermute | solution.py:12
  468.3 14.5 %all-to-all-start = ((bf16[16,2,32,128]{3,2,1,0:T(8,128)(2,1)}), bf16[16,2,32,128]{3,2,1,0:T(8,128)(2,1)S(1)}, u32[]{:S(2)}, u32[]{:S(2)}) async-start(bf16[16,2,32,128]{3,2,1,0:T(8,128)(2,1)} %broadcast_select_fusion.3), calls=%async_computation | async-start | bytes 524288 | tf_op jit(solution)/shard_map/while/body/eval_jaxpr/all_to_all | solution.py:92
  486.7 13.0 %collective-permute-start = (bf16[32,32,128]{2,1,0:T(8,128)(2,1)S(1)}, bf16[32,32,128]{2,1,0:T(8,128)(2,1)S(1)}, u32[]{:S(2)}, u32[]{:S(2)}) collective-permute-start(bf16[32,32,128]{2,1,0:T(8,128)(2,1)S(1)} %get-tuple-element.421), channel_id=1, source_target_pairs={{0,16},{16,32},{32,48},{48,64},{64,80},{80,96},{96,112},{112,128},... | collective-permute-start | bytes 786440 | tf_op jit(solution)/shard_map/while/body/eval_jaxpr/ppermute | solution.py:12
  502.4 14.5 %all-to-all-start = ((bf16[16,2,32,128]{3,2,1,0:T(8,128)(2,1)}), bf16[16,2,32,128]{3,2,1,0:T(8,128)(2,1)S(1)}, u32[]{:S(2)}, u32[]{:S(2)}) async-start(bf16[16,2,32,128]{3,2,1,0:T(8,128)(2,1)} %broadcast_select_fusion.3), calls=%async_computation | async-start | bytes 524288 | tf_op jit(solution)/shard_map/while/body/eval_jaxpr/all_to_all | solution.py:92
  520.8 13.0 %collective-permute-start = (bf16[32,32,128]{2,1,0:T(8,128)(2,1)S(1)}, bf16[32,32,128]{2,1,0:T(8,128)(2,1)S(1)}, u32[]{:S(2)}, u32[]{:S(2)}) collective-permute-start(bf16[32,32,128]{2,1,0:T(8,128)(2,1)S(1)} %get-tuple-element.421), channel_id=1, source_target_pairs={{0,16},{16,32},{32,48},{48,64},{64,80},{80,96},{96,112},{112,128},... | collective-permute-start | bytes 786440 | tf_op jit(solution)/shard_map/while/body/eval_jaxpr/ppermute | solution.py:12
  536.4 14.5 %all-to-all-start = ((bf16[16,2,32,128]{3,2,1,0:T(8,128)(2,1)}), bf16[16,2,32,128]{3,2,1,0:T(8,128)(2,1)S(1)}, u32[]{:S(2)}, u32[]{:S(2)}) async-start(bf16[16,2,32,128]{3,2,1,0:T(8,128)(2,1)} %broadcast_select_fusion.3), calls=%async_computation | async-start | bytes 524288 | tf_op jit(solution)/shard_map/while/body/eval_jaxpr/all_to_all | solution.py:92
  554.8 13.0 %collective-permute-start = (bf16[32,32,128]{2,1,0:T(8,128)(2,1)S(1)}, bf16[32,32,128]{2,1,0:T(8,128)(2,1)S(1)}, u32[]{:S(2)}, u32[]{:S(2)}) collective-permute-start(bf16[32,32,128]{2,1,0:T(8,128)(2,1)S(1)} %get-tuple-element.421), channel_id=1, source_target_pairs={{0,16},{16,32},{32,48},{48,64},{64,80},{80,96},{96,112},{112,128},... | collective-permute-start | bytes 786440 | tf_op jit(solution)/shard_map/while/body/eval_jaxpr/ppermute | solution.py:12
  570.4 14.5 %all-to-all-start = ((bf16[16,2,32,128]{3,2,1,0:T(8,128)(2,1)}), bf16[16,2,32,128]{3,2,1,0:T(8,128)(2,1)S(1)}, u32[]{:S(2)}, u32[]{:S(2)}) async-start(bf16[16,2,32,128]{3,2,1,0:T(8,128)(2,1)} %broadcast_select_fusion.3), calls=%async_computation | async-start | bytes 524288 | tf_op jit(solution)/shard_map/while/body/eval_jaxpr/all_to_all | solution.py:92
  604.5 14.5 %all-to-all-start = ((bf16[16,2,32,128]{3,2,1,0:T(8,128)(2,1)}), bf16[16,2,32,128]{3,2,1,0:T(8,128)(2,1)S(1)}, u32[]{:S(2)}, u32[]{:S(2)}) async-start(bf16[16,2,32,128]{3,2,1,0:T(8,128)(2,1)} %broadcast_select_fusion.3), calls=%async_computation | async-start | bytes 524288 | tf_op jit(solution)/shard_map/while/body/eval_jaxpr/all_to_all | solution.py:92
  622.9 13.0 %collective-permute-start = (bf16[32,32,128]{2,1,0:T(8,128)(2,1)S(1)}, bf16[32,32,128]{2,1,0:T(8,128)(2,1)S(1)}, u32[]{:S(2)}, u32[]{:S(2)}) collective-permute-start(bf16[32,32,128]{2,1,0:T(8,128)(2,1)S(1)} %get-tuple-element.421), channel_id=1, source_target_pairs={{0,16},{16,32},{32,48},{48,64},{64,80},{80,96},{96,112},{112,128},... | collective-permute-start | bytes 786440 | tf_op jit(solution)/shard_map/while/body/eval_jaxpr/ppermute | solution.py:12
  638.5 14.5 %all-to-all-start = ((bf16[16,2,32,128]{3,2,1,0:T(8,128)(2,1)}), bf16[16,2,32,128]{3,2,1,0:T(8,128)(2,1)S(1)}, u32[]{:S(2)}, u32[]{:S(2)}) async-start(bf16[16,2,32,128]{3,2,1,0:T(8,128)(2,1)} %broadcast_select_fusion.3), calls=%async_computation | async-start | bytes 524288 | tf_op jit(solution)/shard_map/while/body/eval_jaxpr/all_to_all | solution.py:92
  672.5 14.5 %all-to-all-start = ((bf16[16,2,32,128]{3,2,1,0:T(8,128)(2,1)}), bf16[16,2,32,128]{3,2,1,0:T(8,128)(2,1)S(1)}, u32[]{:S(2)}, u32[]{:S(2)}) async-start(bf16[16,2,32,128]{3,2,1,0:T(8,128)(2,1)} %broadcast_select_fusion.3), calls=%async_computation | async-start | bytes 524288 | tf_op jit(solution)/shard_map/while/body/eval_jaxpr/all_to_all | solution.py:92
  706.8 31.1 %all-to-all-start.1 = ((bf16[4,16,2,4096]{3,2,0,1:T(2,128)(2,1)}), bf16[4,16,2,4096]{3,2,0,1:T(2,128)(2,1)S(1)}, u32[]{:S(2)}, u32[]{:S(2)}) async-start(bf16[4,16,2,4096]{3,2,0,1:T(2,128)(2,1)} %copy.71), calls=%async_computation.1 | async-start | bytes 2097152 | tf_op jit(solution)/shard_map/all_to_all | solution.py:121
  (25 other events, 237.8 us)
Sparse Core Ops, SparseCore 0:
  13.5 46.4 all-gather.1
